TPU v7x, 32 devices: a whole 2x2x4 slice. The times are simulated.
32 devices in a mesh: dp: 8 (over z, y), tensor: 4 (over x, core).
Axes of the slice: x: 2, y: 2, z: 4, core: 2. Of those that a mesh axis runs over, the one named last changes fastest.
Arguments:
- tokens: bfloat16 [8192, 768], P(('dp', 'tensor')), may hold values from -6 to 6
- cotangent: bfloat16 [8192, 768], P(('dp', 'tensor')), may hold values from -6 to 6
- segments: int32 [8192], P('dp'), may hold values from 0 to 95, as said below
- lengths: int32 [32, 2], P('dp'), may hold values from 2 to 197, as said below
- rel_index: int32 [8192, 256], P('dp'), may hold values from 0 to 731, as said below
- w_qkv: bfloat16 [2, 768, 3, 768], P(None, None, None, 'tensor'), may hold values from -0.21875 to 0.21875
- qv_bias: bfloat16 [2, 2, 768], P(None, None, 'tensor'), may hold values from -3 to 3
- w_out: bfloat16 [2, 768, 768], P(None, 'tensor'), may hold values from -0.875 to 0.875
- w_fc1: bfloat16 [2, 768, 3072], P(None, None, 'tensor'), may hold values from -0.21875 to 0.21875
- fc1_bias: bfloat16 [2, 3072], P(None, 'tensor'), may hold values from -3 to 3
- w_fc2: bfloat16 [2, 3072, 768], P(None, 'tensor'), may hold values from -0.109375 to 0.109375
- rel_table: bfloat16 [2, 732, 12], P(None, None, 'tensor'), may hold values from -5 to 5
- ln_gain: float32 [2, 2, 768], replicated, may hold values from 0.25 to 1.75
- ln_bias: float32 [2, 2, 768], replicated, may hold values from -2 to 2
- layer_scale: float32 [2, 2, 768], replicated, may hold values from 0.25 to 1.75
- row_bias: float32 [2, 2, 768], replicated, may hold values from -2 to 2
Outputs:
- result: bfloat16 [8192, 768], P(('dp', 'tensor'))
- d_tokens: float32 [8192, 768], P(('dp', 'tensor'))
- d_w_qkv: float32 [2, 768, 3, 768], P(None, None, None, 'tensor')
- d_qv_bias: float32 [2, 2, 768], P(None, None, 'tensor')
- d_w_out: float32 [2, 768, 768], P(None, 'tensor')
- d_w_fc1: float32 [2, 768, 3072], P(None, None, 'tensor')
- d_fc1_bias: float32 [2, 3072], P(None, 'tensor')
- d_w_fc2: float32 [2, 3072, 768], P(None, 'tensor')
- d_rel_table: float32 [2, 732, 12], P(None, None, 'tensor')
- d_ln_gain: float32 [2, 2, 768], replicated
- d_ln_bias: float32 [2, 2, 768], replicated
- d_layer_scale: float32 [2, 2, 768], replicated
- d_row_bias: float32 [2, 2, 768], replicated
Inputs may be any that keep to these rules, and one draw needn't show every extreme that they name: `segments`: rows with equal ids belong to one image, or to the padding that ends one bin of 256 rows. Bin b holds rows of id 3 b (its first image), then 3 b + 1 (its second image), then one or more rows of id 3 b + 2 (padding). `lengths`: the rows of a bin's first and second image, in the order of segments; an image of r by c patches has r c + 1 rows, its class token first, then its patches row by row; a bin's two lengths sum to 255 or less. `rel_index`: for rows i and j of one image: (dr + 13) * 27 + dc + 13 for two patches whose row and column offsets are dr and dc, 729 from the class token to a patch, 730 from a patch to the class token, 731 for the class token with itself. Other entries are arbitrary.
All inputs are finite; a program needn't handle non-finite values.
Results may differ from a plain program's by a relative error of at most 0.023.
Values may be sent and summed in bfloat16 or wider, within the bound.
A program may use at most 128 MiB of HBM per device.

v0:
```python
import math
import jax
import jax.numpy as jnp
from jax import lax
from jax.sharding import PartitionSpec as P

HEAD_DIM = 64


def norm_rows(stream, norm_gain, norm_shift):
    center = stream - jnp.mean(stream, -1, keepdims=True)
    inverse = lax.rsqrt(jnp.mean(center * center, -1, keepdims=True) + 1e-06)
    normal = center * inverse
    return (normal * norm_gain + norm_shift, normal, inverse)


def norm_back(gradient, normal, inverse, norm_gain):
    scaled = gradient * norm_gain
    centered = (
        scaled
        - jnp.mean(scaled, -1, keepdims=True)
        - normal * jnp.mean(scaled * normal, -1, keepdims=True)
    )
    return (inverse * centered, jnp.sum(gradient * normal, 0), jnp.sum(gradient, 0))


def gelu_slope(values):
    return (
        0.5 * (1.0 + lax.erf(values * 0.7071067811865476))
        + values * jnp.exp(-0.5 * values * values) * 0.3989422804014327
    )


def contract_rows(left_side, right_side):
    return lax.dot_general(
        left_side, right_side, (((0,), (0,)), ((), ())), preferred_element_type=jnp.float32
    )


def times_transposed(left_side, right_side):
    return lax.dot_general(
        left_side, right_side, (((1,), (1,)), ((), ())), preferred_element_type=jnp.float32
    )


def block_rows(amount, bin_rows):
    return math.gcd(amount, max(1, 16384 // bin_rows))


def look_up(index_rows, table_used):
    amount, bin_rows = index_rows.shape
    layer_count, entries, head_count = table_used.shape
    step_rows = block_rows(amount, bin_rows)
    index_blocks = index_rows.reshape(amount // step_rows, step_rows * bin_rows)
    columns = jnp.transpose(table_used, (0, 2, 1)).reshape(layer_count * head_count, entries)
    table_rows = lax.broadcasted_iota(jnp.int32, (entries, 1), 0)

    def one_block(index_flat):
        onehot = (table_rows == index_flat[None, :]).astype(jnp.bfloat16)
        return jnp.dot(columns, onehot, preferred_element_type=jnp.float32).astype(jnp.bfloat16)

    looked = lax.map(one_block, index_blocks)
    looked = jnp.transpose(looked, (1, 0, 2)).reshape(
        layer_count, head_count, amount // bin_rows, bin_rows, bin_rows
    )
    return jnp.transpose(looked, (0, 2, 1, 3, 4))


def table_grad(index_rows, score_grads, entries):
    amount, bin_rows = index_rows.shape
    layer_count, bin_total, head_count = (
        score_grads.shape[0],
        score_grads.shape[1],
        score_grads.shape[2],
    )
    step_rows = block_rows(amount, bin_rows)
    step_count = amount // step_rows
    index_blocks = index_rows.reshape(step_count, step_rows * bin_rows)
    pieces = jnp.transpose(score_grads, (0, 2, 1, 3, 4)).reshape(
        layer_count * head_count, step_count, step_rows * bin_rows
    )
    pieces = jnp.transpose(pieces, (1, 0, 2))
    table_rows = lax.broadcasted_iota(jnp.int32, (entries, 1), 0)

    def add_block(totals, element):
        onehot = (table_rows == element[0][None, :]).astype(jnp.bfloat16)
        return (totals + times_transposed(element[1], onehot), None)

    totals, unused_out = lax.scan(
        add_block,
        jnp.zeros((layer_count * head_count, entries), jnp.float32),
        (index_blocks, pieces),
    )
    return jnp.transpose(totals.reshape(layer_count, head_count, entries), (0, 2, 1))


def attend_scores(queries, key_rows, position_bias, same_image, head_count, score_scale):
    local_width = queries.shape[1]
    blocked = (same_image.shape[0], same_image.shape[1], head_count, local_width // head_count)
    products = jnp.einsum(
        "bqhd,bkhd->bhqk",
        queries.reshape(blocked),
        key_rows.reshape(blocked),
        preferred_element_type=jnp.float32,
    )
    return jnp.where(
        same_image[:, None],
        products * score_scale + position_bias.astype(jnp.float32),
        -1000000000.0,
    )


def attend(queries, key_rows, values, position_bias, same_image, head_count, score_scale):
    scores = attend_scores(queries, key_rows, position_bias, same_image, head_count, score_scale)
    highest = jnp.max(scores, -1, keepdims=True)
    powers = jnp.exp(scores - highest)
    totals = jnp.sum(powers, -1, keepdims=True)
    weights = (powers / totals).astype(jnp.bfloat16)
    local_width = queries.shape[1]
    blocked = (same_image.shape[0], same_image.shape[1], head_count, local_width // head_count)
    mixture = jnp.einsum(
        "bhqk,bkhd->bqhd", weights, values.reshape(blocked), preferred_element_type=jnp.float32
    )
    return (mixture.reshape(queries.shape).astype(jnp.bfloat16), highest + jnp.log(totals))


def attend_back(
    queries,
    key_rows,
    values,
    position_bias,
    same_image,
    log_totals,
    grad_mix,
    head_count,
    score_scale,
):
    scores = attend_scores(queries, key_rows, position_bias, same_image, head_count, score_scale)
    weights = jnp.exp(scores - log_totals)
    local_width = queries.shape[1]
    blocked = (same_image.shape[0], same_image.shape[1], head_count, local_width // head_count)
    grad_blocked = grad_mix.reshape(blocked)
    grad_weights = jnp.einsum(
        "bqhd,bkhd->bhqk", grad_blocked, values.reshape(blocked), preferred_element_type=jnp.float32
    )
    grad_values = jnp.einsum(
        "bhqk,bqhd->bkhd",
        weights.astype(jnp.bfloat16),
        grad_blocked,
        preferred_element_type=jnp.float32,
    )
    centered = jnp.sum(weights * grad_weights, -1, keepdims=True)
    grad_scores = (weights * (grad_weights - centered)).astype(jnp.bfloat16)
    grad_query = (
        jnp.einsum(
            "bhqk,bkhd->bqhd",
            grad_scores,
            key_rows.reshape(blocked),
            preferred_element_type=jnp.float32,
        )
        * score_scale
    )
    grad_key = (
        jnp.einsum(
            "bhqk,bqhd->bkhd",
            grad_scores,
            queries.reshape(blocked),
            preferred_element_type=jnp.float32,
        )
        * score_scale
    )
    flat_shape = queries.shape
    return (
        grad_query.reshape(flat_shape).astype(jnp.bfloat16),
        grad_key.reshape(flat_shape).astype(jnp.bfloat16),
        grad_values.reshape(flat_shape).astype(jnp.bfloat16),
        grad_scores,
    )


def per_device(
    tokens,
    cotangent,
    segments,
    lengths,
    rel_index,
    w_qkv,
    qv_bias,
    w_out,
    w_fc1,
    fc1_bias,
    w_fc2,
    rel_table,
    ln_gain,
    ln_bias,
    layer_scale,
    row_bias,
):
    own_rows, width = tokens.shape
    group_rows, bin_rows = rel_index.shape
    layer_count = w_qkv.shape[0]
    entries = rel_table.shape[1]
    place = lax.axis_index("tensor")
    score_scale = float(HEAD_DIM) ** (-0.5)
    totals = jnp.sum(lengths, 1)
    inside = jnp.arange(group_rows) % bin_rows < jnp.repeat(totals, bin_rows)
    valid = lax.dynamic_slice_in_dim(inside, place * own_rows, own_rows)[:, None]
    proj_qkv, proj_bias, proj_out, proj_up, up_bias, proj_down, table_used = (
        w_qkv,
        qv_bias,
        w_out,
        w_fc1,
        fc1_bias,
        w_fc2,
        rel_table,
    )
    head_count = table_used.shape[2]
    local_width = proj_qkv.shape[3]
    bin_total = rel_index.shape[0] // bin_rows
    seg_bins = segments.reshape(bin_total, bin_rows)
    same_image = seg_bins[:, :, None] == seg_bins[:, None, :]
    position_bias = look_up(rel_index, table_used)

    def spread_rows(values):
        return lax.all_gather(values, "tensor", axis=0, tiled=True)

    def spread_grads(values):
        return lax.all_gather(values, "tensor", axis=0, tiled=True)

    def project_rows(left_side, right_side):
        return lax.psum_scatter(
            jnp.dot(left_side, right_side, preferred_element_type=jnp.float32).astype(jnp.bfloat16),
            "tensor",
            scatter_dimension=0,
            tiled=True,
        ).astype(jnp.float32)

    def project_grads(left_side, right_side):
        return lax.psum_scatter(
            times_transposed(left_side, right_side).astype(jnp.bfloat16),
            "tensor",
            scatter_dimension=0,
            tiled=True,
        ).astype(jnp.float32)

    stream = tokens.astype(jnp.float32)
    kept_state = []
    for layer_at in range(layer_count):
        layer_qkv = proj_qkv[layer_at].reshape(width, 3 * local_width)
        normed, normal_a, inverse_a = norm_rows(stream, ln_gain[layer_at, 0], ln_bias[layer_at, 0])
        spread_a = spread_rows(normed.astype(jnp.bfloat16))
        mixed_proj = jnp.dot(spread_a, layer_qkv, preferred_element_type=jnp.float32).reshape(
            -1, 3, local_width
        )
        biases = proj_bias[layer_at].astype(jnp.float32)
        queries = (mixed_proj[:, 0] + biases[0]).astype(jnp.bfloat16)
        key_rows = mixed_proj[:, 1].astype(jnp.bfloat16)
        values = (mixed_proj[:, 2] + biases[1]).astype(jnp.bfloat16)
        mixture, log_totals = attend(
            queries, key_rows, values, position_bias[layer_at], same_image, head_count, score_scale
        )
        branch_a = project_rows(mixture, proj_out[layer_at]) + row_bias[layer_at, 0]
        middle = stream + layer_scale[layer_at, 0] * branch_a
        normed_b, normal_b, inverse_b = norm_rows(
            middle, ln_gain[layer_at, 1], ln_bias[layer_at, 1]
        )
        spread_b = spread_rows(normed_b.astype(jnp.bfloat16))
        hidden = jnp.dot(spread_b, proj_up[layer_at], preferred_element_type=jnp.float32) + up_bias[
            layer_at
        ].astype(jnp.float32)
        active = jax.nn.gelu(hidden, approximate=False).astype(jnp.bfloat16)
        branch_b = project_rows(active, proj_down[layer_at]) + row_bias[layer_at, 1]
        kept_state.append(
            (
                normal_a,
                inverse_a,
                spread_a,
                queries,
                key_rows,
                values,
                mixture,
                log_totals,
                branch_a,
                normal_b,
                inverse_b,
                spread_b,
                hidden,
                active,
                branch_b,
            )
        )
        stream = middle + layer_scale[layer_at, 1] * branch_b
    result = jnp.where(valid, stream, 0.0).astype(jnp.bfloat16)
    gradient = jnp.where(valid, cotangent.astype(jnp.float32), 0.0)
    list_qkv = [None] * layer_count
    list_qvb = [None] * layer_count
    list_out = [None] * layer_count
    list_up = [None] * layer_count
    list_upb = [None] * layer_count
    list_down = [None] * layer_count
    list_scores = [None] * layer_count
    list_gain = [None] * layer_count
    list_shift = [None] * layer_count
    list_scale = [None] * layer_count
    list_rowb = [None] * layer_count
    for layer_at in reversed(range(layer_count)):
        (
            normal_a,
            inverse_a,
            spread_a,
            queries,
            key_rows,
            values,
            mixture,
            log_totals,
            branch_a,
            normal_b,
            inverse_b,
            spread_b,
            hidden,
            active,
            branch_b,
        ) = kept_state[layer_at]
        scale_b = jnp.sum(gradient * branch_b, 0)
        rowb_b = layer_scale[layer_at, 1] * jnp.sum(gradient, 0)
        spread_down = spread_grads((gradient * layer_scale[layer_at, 1]).astype(jnp.bfloat16))
        list_down[layer_at] = contract_rows(active, spread_down)
        grad_active = times_transposed(spread_down, proj_down[layer_at])
        grad_hidden = (grad_active * gelu_slope(hidden)).astype(jnp.bfloat16)
        list_upb[layer_at] = jnp.sum(grad_hidden.astype(jnp.float32), 0)
        list_up[layer_at] = contract_rows(spread_b, grad_hidden)
        back_b, gain_b, shift_b = norm_back(
            project_grads(grad_hidden, proj_up[layer_at]), normal_b, inverse_b, ln_gain[layer_at, 1]
        )
        gradient = gradient + back_b
        scale_a = jnp.sum(gradient * branch_a, 0)
        rowb_a = layer_scale[layer_at, 0] * jnp.sum(gradient, 0)
        spread_attn = spread_grads((gradient * layer_scale[layer_at, 0]).astype(jnp.bfloat16))
        list_out[layer_at] = contract_rows(mixture, spread_attn)
        grad_mix = times_transposed(spread_attn, proj_out[layer_at]).astype(jnp.bfloat16)
        grad_query, grad_key, grad_value, grad_scores = attend_back(
            queries,
            key_rows,
            values,
            position_bias[layer_at],
            same_image,
            log_totals,
            grad_mix,
            head_count,
            score_scale,
        )
        list_scores[layer_at] = grad_scores
        list_qvb[layer_at] = jnp.stack(
            [jnp.sum(grad_query.astype(jnp.float32), 0), jnp.sum(grad_value.astype(jnp.float32), 0)]
        )
        grad_proj = jnp.stack([grad_query, grad_key, grad_value], 1).reshape(-1, 3 * local_width)
        list_qkv[layer_at] = contract_rows(spread_a, grad_proj).reshape(width, 3, local_width)
        back_a, gain_a, shift_a = norm_back(
            project_grads(grad_proj, proj_qkv[layer_at].reshape(width, 3 * local_width)),
            normal_a,
            inverse_a,
            ln_gain[layer_at, 0],
        )
        gradient = gradient + back_a
        list_gain[layer_at] = jnp.stack([gain_a, gain_b])
        list_shift[layer_at] = jnp.stack([shift_a, shift_b])
        list_scale[layer_at] = jnp.stack([scale_a, scale_b])
        list_rowb[layer_at] = jnp.stack([rowb_a, rowb_b])
    qkv_all = jnp.stack(list_qkv)
    qvb_all = jnp.stack(list_qvb)
    out_all = jnp.stack(list_out)
    up_all = jnp.stack(list_up)
    upb_all = jnp.stack(list_upb)
    down_all = jnp.stack(list_down)
    table_all = table_grad(rel_index, jnp.stack(list_scores), entries)
    qkv_all, qvb_all, out_all, up_all, upb_all, down_all, table_all = lax.psum(
        (qkv_all, qvb_all, out_all, up_all, upb_all, down_all, table_all), "dp"
    )
    gain_all, shift_all, scale_all, rowb_all = lax.psum(
        (jnp.stack(list_gain), jnp.stack(list_shift), jnp.stack(list_scale), jnp.stack(list_rowb)),
        ("dp", "tensor"),
    )
    return (
        result,
        gradient,
        qkv_all,
        qvb_all,
        out_all,
        up_all,
        upb_all,
        down_all,
        table_all,
        gain_all,
        shift_all,
        scale_all,
        rowb_all,
    )


def solution(mesh):
    in_specs = (
        P(("dp", "tensor"), None),
        P(("dp", "tensor"), None),
        P("dp"),
        P("dp", None),
        P("dp", None),
        P(None, None, None, "tensor"),
        P(None, None, "tensor"),
        P(None, "tensor", None),
        P(None, None, "tensor"),
        P(None, "tensor"),
        P(None, "tensor", None),
        P(None, None, "tensor"),
        P(),
        P(),
        P(),
        P(),
    )
    out_specs = (
        P(("dp", "tensor"), None),
        P(("dp", "tensor"), None),
        P(None, None, None, "tensor"),
        P(None, None, "tensor"),
        P(None, "tensor", None),
        P(None, None, "tensor"),
        P(None, "tensor"),
        P(None, "tensor", None),
        P(None, None, "tensor"),
        P(),
        P(),
        P(),
        P(),
    )
    return jax.shard_map(
        per_device, mesh=mesh, in_specs=in_specs, out_specs=out_specs, check_vma=False
    )
```

profile of v0, /device:TPU:0, one launch (start us, length us, event | category | flops | bytes accessed | tf_op | source)
XLA Modules:
  0.0 1150.7 jit_solution(10076995145062278454)
XLA Ops:
  15.4 128.6 %while.22 = (s32[]{:T(128)}, bf16[16,6,16384]{2,1,0:T(8,128)(2,1)}, s32[16,16384]{1,0:T(8,128)S(1)}, bf16[6,732]{1,0:T(8,128)(2,1)S(1)}, s32[]{:T(128)}) while((s32[]{:T(128)}, bf16[16,6,16384]{2,1,0:T(8,128)(2,1)}, s32[16,16384]{1,0:T(8,128)S(1)}, bf16[6,732]{1,0:T(8,128)(2,1)S(1)}, s32[]{:T(128)}) %tuple.112), condition=%wide.region_4.5_spmd.clone, body=%wide.region_3.4_spmd.clone.sunk | while | flops 156008448 | bytes 467613 | solution.py:62
  15.5 8.0 fusion.241
  23.5 8.0 fusion.241
  31.5 8.0 fusion.241
  39.6 8.0 fusion.241
  47.6 8.0 fusion.241
  55.6 8.0 fusion.241
  63.7 8.0 fusion.241
  71.7 8.0 fusion.241
  79.8 8.0 fusion.241
  87.8 8.0 fusion.241
  95.8 8.0 fusion.241
  103.9 8.0 fusion.241
  111.9 8.0 fusion.241
  119.9 8.0 fusion.241
  128.0 8.0 fusion.241
  136.0 8.0 fusion.241
  145.4 3.9 copy.54
  152.7 5.0 copy.55
  174.2 29.5 %reduce-scatter.9.cloned.1.call-done = bf16[256,768]{1,0:T(8,128)(2,1)} async-done(((bf16[1024,768]{1,0:T(8,128)(2,1)}), bf16[256,768]{1,0:T(8,128)(2,1)}) %reduce-scatter.9.cloned.1.call-update) | async-done | bytes 393232 | tf_op jit(solution)/shard_map/reduce_scatter | solution.py:231
  210.2 18.4 %all-gather.11.cloned.1.call-done = bf16[1024,768]{1,0:T(8,128)(2,1)} async-done(((bf16[256,768]{1,0:T(8,128)(2,1)}), bf16[1024,768]{1,0:T(8,128)(2,1)}) %all-gather.11.cloned.1.call-update) | async-done | bytes 1572880 | tf_op jit(solution)/shard_map/all_gather | solution.py:225
  228.6 11.0 fusion.17
  243.3 28.3 %reduce-scatter.11.cloned.1.call-done = bf16[256,768]{1,0:T(8,128)(2,1)} async-done(((bf16[1024,768]{1,0:T(8,128)(2,1)}), bf16[256,768]{1,0:T(8,128)(2,1)}) %reduce-scatter.11.cloned.1.call-update) | async-done | bytes 393232 | tf_op jit(solution)/shard_map/reduce_scatter | solution.py:231
  275.6 11.0 reduce-scatter.13.cloned.1.call-start
  289.3 6.2 all-gather.13.cloned.1.call-done
  315.4 28.3 %reduce-scatter.13.cloned.1.call-done = bf16[256,768]{1,0:T(8,128)(2,1)} async-done(((bf16[1024,768]{1,0:T(8,128)(2,1)}), bf16[256,768]{1,0:T(8,128)(2,1)}) %reduce-scatter.13.cloned.1.call-update) | async-done | bytes 393232 | tf_op jit(solution)/shard_map/reduce_scatter | solution.py:231
  351.1 16.4 %all-gather.15.cloned.1.call-done = bf16[1024,768]{1,0:T(8,128)(2,1)} async-done(((bf16[256,768]{1,0:T(8,128)(2,1)}), bf16[1024,768]{1,0:T(8,128)(2,1)}) %all-gather.15.cloned.1.call-update) | async-done | bytes 1572880 | tf_op jit(solution)/shard_map/all_gather | solution.py:225
  367.5 11.2 fusion.20
  378.7 10.2 all-gather.17.cloned.1.call-done
  388.9 5.6 convert_reduce_fusion
  398.3 4.3 convolution_convert_fusion.4
  402.7 23.9 %reduce-scatter.17.cloned.1.call-done = bf16[256,768]{1,0:T(8,128)(2,1)} async-done(((bf16[1024,768]{1,0:T(8,128)(2,1)}), bf16[256,768]{1,0:T(8,128)(2,1)}) %reduce-scatter.17.cloned.1.call-update) | async-done | bytes 393232 | tf_op jit(solution)/shard_map/reduce_scatter | solution.py:239
  430.0 27.2 %reduce-scatter.15.cloned.1.call-done = bf16[256,768]{1,0:T(8,128)(2,1)} async-done(((bf16[1024,768]{1,0:T(8,128)(2,1)}), bf16[256,768]{1,0:T(8,128)(2,1)}) %reduce-scatter.15.cloned.1.call-update) | async-done | bytes 393232 | tf_op jit(solution)/shard_map/reduce_scatter | solution.py:231
  466.4 15.9 %all-gather.19.cloned.1.call-done = bf16[1024,768]{1,0:T(8,128)(2,1)} async-done(((bf16[256,768]{1,0:T(8,128)(2,1)}), bf16[1024,768]{1,0:T(8,128)(2,1)}) %all-gather.19.cloned.1.call-update) | async-done | bytes 1572880 | tf_op jit(solution)/shard_map/all_gather | solution.py:228
  516.0 28.3 %reduce-scatter.19.cloned.1.call-done = bf16[256,768]{1,0:T(8,128)(2,1)} async-done(((bf16[1024,768]{1,0:T(8,128)(2,1)}), bf16[256,768]{1,0:T(8,128)(2,1)}) %reduce-scatter.19.cloned.1.call-update) | async-done | bytes 393232 | tf_op jit(solution)/shard_map/reduce_scatter | solution.py:239
  550.9 19.8 %all-gather.21.cloned.1.call-done = bf16[1024,768]{1,0:T(8,128)(2,1)} async-done(((bf16[256,768]{1,0:T(8,128)(2,1)}), bf16[1024,768]{1,0:T(8,128)(2,1)}) %all-gather.21.cloned.1.call-update) | async-done | bytes 1572880 | tf_op jit(solution)/shard_map/all_gather | solution.py:228
  570.7 5.6 convert_reduce_fusion.1
  580.1 28.3 %reduce-scatter.21.cloned.1.call-done = bf16[256,768]{1,0:T(8,128)(2,1)} async-done(((bf16[1024,768]{1,0:T(8,128)(2,1)}), bf16[256,768]{1,0:T(8,128)(2,1)}) %reduce-scatter.21.cloned.1.call-update) | async-done | bytes 393232 | tf_op jit(solution)/shard_map/reduce_scatter | solution.py:239
  617.0 4.9 convolution_bitcast_fusion.2
  631.0 4.1 fusion.72
  670.7 4.7 copy.81
  675.5 4.2 reshape.401
  679.7 3.9 copy.82
  690.2 169.5 %while.23 = (s32[]{:T(128)}, f32[6,732]{1,0:T(8,128)S(1)}, bf16[16,6,16384]{2,1,0:T(8,128)(2,1)}, s32[16,16384]{1,0:T(8,128)}, s32[]{:T(128)}, /*index=5*/s32[]{:T(128)}) while((s32[]{:T(128)}, f32[6,732]{1,0:T(8,128)S(1)}, bf16[16,6,16384]{2,1,0:T(8,128)(2,1)}, s32[16,16384]{1,0:T(8,128)}, s32[]{:T(128)}, ...), condition=%wide.region_46.47_spmd.clone, body=%wide.region_45.46_spmd.clone.sunk | while | flops 155918912 | bytes 493983 | solution.py:89
  691.5 9.5 fusion.243
  702.1 9.5 fusion.243
  712.7 9.5 fusion.243
  723.3 9.5 fusion.243
  733.8 9.5 fusion.243
  744.4 9.5 fusion.243
  755.0 9.5 fusion.243
  765.6 9.5 fusion.243
  776.1 9.5 fusion.243
  786.7 9.5 fusion.243
  797.3 9.5 fusion.243
  807.9 9.5 fusion.243
  818.4 9.5 fusion.243
  829.0 9.5 fusion.243
  839.6 9.5 fusion.243
  850.2 9.5 fusion.243
  859.9 40.7 %all-reduce.1 = (f32[2,2,192]{2,1,0:T(2,128)}, f32[2,768]{1,0:T(2,128)}, f32[2,732,3]{1,2,0:T(4,128)S(1)}) all-reduce(f32[2,2,192]{2,1,0:T(2,128)S(1)} %pad_maximum_fusion.9, f32[2,768]{1,0:T(2,128)S(1)} %copy-done.67, f32[2,732,3]{1,2,0:T(4,128)S(1)} %bitcast.278), channel_id=1, replica_groups=mesh['dp'=8,'tensor'=4] {'dp'}, use_global_device_ids=true, to_apply=%region_38.39 | all-reduce | flops 6696 | bytes 53568 | tf_op jit(solution)/shard_map/psum | solution.py:376
  902.8 40.4 %all-reduce = (f32[2,2,768]{2,1,0:T(2,128)}, f32[2,2,768]{2,1,0:T(2,128)}, f32[2,2,768]{2,1,0:T(2,128)}, f32[2,2,768]{2,1,0:T(2,128)}) all-reduce(f32[2,2,768]{2,1,0:T(2,128)S(1)} %pad_maximum_fusion.4, f32[2,2,768]{2,1,0:T(2,128)S(1)} %pad_maximum_fusion.5, ...), channel_id=1, replica_groups=mesh['dp'=8,'tensor'=4] {'dp','tensor'}, use_global_device_ids=true, to_apply=%region_52.53 | all-reduce | flops 12288 | bytes 98304 | tf_op jit(solution)/shard_map/psum | solution.py:379
  945.4 187.2 %all-reduce.5.cloned.1.call-done = (f32[2,768,3,192]{1,3,2,0:T(8,128)}, f32[2,192,768]{2,1,0:T(8,128)}, f32[2,768,768]{2,1,0:T(8,128)}, f32[2,768,768]{2,1,0:T(8,128)}) async-done(((f32[2,768,3,192]{1,3,2,0:T(8,128)}, f32[2,192,768]{2,1,0:T(8,128)}, f32[2,768,768]{2,1,0:T(8,128)}, f32[2,768,768]{2,1,0:T(8,128)}), (f32[2,768,3,192]{1,3,2,0:T(8,128)}, f32[2,192,768]{2,1,0:T(8,128)}, f32[2,768,768]{2,1,0:T(8,128)}, ...) | async-done | bytes 14155792 | tf_op jit(solution)/shard_map/psum | solution.py:376
  1132.6 4.4 copy.176
  (487 shorter events, 222.8 us)
Async XLA Ops:
  7.2 340.6 %copy-start = (s32[4,2]{0,1:T(2,128)S(1)}, s32[4,2]{0,1:T(2,128)}, u32[]{:S(2)}) copy-start(s32[4,2]{0,1:T(2,128)} %param.23) | copy-start | bytes 100
  7.2 151.4 %all-gather.9.cloned.1.call-start = ((), (), s32[]{:S(2)}) async-start(), calls=%async_computation.8 | async-start | bytes 1966080 | tf_op jit(solution)/shard_map/all_gather | solution.py:225
  8.4 4.8 copy-start.57
  13.1 190.5 %reduce-scatter.9.cloned.1.call-start = ((), (), s32[]{:S(2)}) async-start(), calls=%async_computation.9 | async-start | bytes 1966080 | tf_op jit(solution)/shard_map/reduce_scatter | solution.py:231
  15.4 128.6 %copy-start.102 = (s32[1024]{0:T(1024)S(1)}, s32[1024]{0:T(1024)}, u32[]{:S(2)}) copy-start(s32[1024]{0:T(1024)} %param.22) | copy-start | bytes 12292
  15.4 128.6 %copy-start.103 = (bf16[2,2,192]{2,1,0:T(2,128)(2,1)S(1)}, bf16[2,2,192]{2,1,0:T(2,128)(2,1)}, u32[]{:S(2)}) copy-start(bf16[2,2,192]{2,1,0:T(2,128)(2,1)} %param.26) | copy-start | bytes 4612
  144.8 20.1 %copy-start.91 = (f32[3,64]{1,0:T(4,128)}, f32[3,64]{1,0:T(4,128)S(1)}, u32[]{:S(2)}) copy-start(f32[3,64]{1,0:T(4,128)S(1)} %add.307) | copy-start | bytes 2308
  152.7 5.9 copy-start.30
  169.6 34.0 %copy-start.4 = (bf16[256,768]{1,0:T(8,128)(2,1)S(1)}, bf16[256,768]{1,0:T(8,128)(2,1)}, u32[]{:S(2)}) copy-start(bf16[256,768]{1,0:T(8,128)(2,1)} %param.20) | copy-start | bytes 1179652
  172.6 56.0 %all-gather.11.cloned.1.call-start = ((), (), s32[]{:S(2)}) async-start(), calls=%async_computation.10 | async-start | bytes 1966080 | tf_op jit(solution)/shard_map/all_gather | solution.py:225
  208.8 62.8 %reduce-scatter.11.cloned.1.call-start = ((), (), s32[]{:S(2)}) async-start(), calls=%async_computation.11 | async-start | bytes 1966080 | tf_op jit(solution)/shard_map/reduce_scatter | solution.py:231
  228.6 12.1 %copy-start.105 = (bf16[2,768,768]{2,1,0:T(8,128)(2,1)S(1)}, bf16[2,768,768]{2,1,0:T(8,128)(2,1)}, u32[]{:S(2)}) copy-start(bf16[2,768,768]{2,1,0:T(8,128)(2,1)} %param.30) | copy-start | bytes 7077892
  243.3 52.2 %all-gather.13.cloned.1.call-start = ((), (), s32[]{:S(2)}) async-start(), calls=%async_computation.12 | async-start | bytes 1966080 | tf_op jit(solution)/shard_map/all_gather | solution.py:225
  275.6 68.1 %reduce-scatter.13.cloned.1.call-start = ((), (), s32[]{:S(2)}) async-start(), calls=%async_computation.13 | async-start | bytes 1966080 | tf_op jit(solution)/shard_map/reduce_scatter | solution.py:231
  315.4 52.1 %all-gather.15.cloned.1.call-start = ((), (), s32[]{:S(2)}) async-start(), calls=%async_computation.14 | async-start | bytes 1966080 | tf_op jit(solution)/shard_map/all_gather | solution.py:225
  347.7 41.2 %all-gather.17.cloned.1.call-start = ((), (), s32[]{:S(2)}) async-start(), calls=%async_computation.16 | async-start | bytes 1966080 | tf_op jit(solution)/shard_map/all_gather | solution.py:228
  349.1 18.4 %copy-start.104 = (pred[256]{0:T(512)(128)(4,1)}, pred[256]{0:T(512)(128)(4,1)S(1)}, u32[]{:S(2)}) copy-start(pred[256]{0:T(512)(128)(4,1)S(1)} %dynamic_slice.14) | copy-start | bytes 772
  351.1 75.5 %reduce-scatter.17.cloned.1.call-start = ((), (), s32[]{:S(2)}) async-start(), calls=%async_computation.17 | async-start | bytes 1966080 | tf_op jit(solution)/shard_map/reduce_scatter | solution.py:239
  367.5 21.4 %copy-start.100 = (f32[768]{0:T(1024)S(1)}, f32[768]{0:T(1024)}, u32[]{:S(2)}) copy-start(f32[768]{0:T(1024)} %get-tuple-element.153) | copy-start | bytes 9220
  388.9 6.7 copy-start.106
  398.3 58.9 %reduce-scatter.15.cloned.1.call-start = ((), (), s32[]{:S(2)}) async-start(), calls=%async_computation.15 | async-start | bytes 1966080 | tf_op jit(solution)/shard_map/reduce_scatter | solution.py:231
  398.3 28.3 %copy-start.46 = (f32[768]{0:T(1024)S(1)}, f32[768]{0:T(1024)}, u32[]{:S(2)}) copy-start(f32[768]{0:T(1024)} %get-tuple-element.235) | copy-start | bytes 9220
  402.6 79.7 %all-gather.19.cloned.1.call-start = ((), (), s32[]{:S(2)}) async-start(), calls=%async_computation.18 | async-start | bytes 1966080 | tf_op jit(solution)/shard_map/all_gather | solution.py:228
  457.2 4.6 copy-start.56
  462.6 81.7 %reduce-scatter.19.cloned.1.call-start = ((), (), s32[]{:S(2)}) async-start(), calls=%async_computation.19 | async-start | bytes 1966080 | tf_op jit(solution)/shard_map/reduce_scatter | solution.py:239
  466.4 24.2 %copy-start.99 = (f32[3,64]{1,0:T(4,128)S(1)}, f32[3,64]{1,0:T(4,128)}, u32[]{:S(2)}) copy-start(f32[3,64]{1,0:T(4,128)} %add.331) | copy-start | bytes 2308
  512.2 32.1 %copy-start.45 = (f32[768]{0:T(1024)S(1)}, f32[768]{0:T(1024)}, u32[]{:S(2)}) copy-start(f32[768]{0:T(1024)} %get-tuple-element.232) | copy-start | bytes 9220
  515.9 54.8 %all-gather.21.cloned.1.call-start = ((), (), s32[]{:S(2)}) async-start(), calls=%async_computation.20 | async-start | bytes 1966080 | tf_op jit(solution)/shard_map/all_gather | solution.py:228
  544.3 5.8 copy-start.55
  550.9 57.5 %reduce-scatter.21.cloned.1.call-start = ((), (), s32[]{:S(2)}) async-start(), calls=%async_computation.21 | async-start | bytes 1966080 | tf_op jit(solution)/shard_map/reduce_scatter | solution.py:239
  570.7 6.7 copy-start.107
  577.4 30.9 %copy-start.60 = (f32[256]{0:T(256)S(1)}, f32[256]{0:T(256)}, u32[]{:S(2)}) copy-start(f32[256]{0:T(256)} %copy-done.59) | copy-start | bytes 3076
  580.0 56.3 %all-gather.23.cloned.1.call-start = ((), (), s32[]{:S(2)}) async-start(), calls=%async_computation.22 | async-start | bytes 1966080 | tf_op jit(solution)/shard_map/all_gather | solution.py:228
  614.8 286.4 %reduce-scatter.23.cloned.1.call-start = ((), (), s32[]{:S(2)}) async-start(), calls=%async_computation.23 | async-start | bytes 1966080 | tf_op jit(solution)/shard_map/reduce_scatter | solution.py:239
  617.0 4.9 copy-start.110
  617.0 4.9 copy-start.112
  631.0 4.1 copy-start.85
  631.0 4.1 copy-start.86
  631.0 4.1 copy-start.84
  631.0 4.8 copy-start.89
  631.0 5.4 copy-start.101
  636.3 7.3 copy-start.97
  654.3 478.3 %all-reduce.5.cloned.1.call-start = ((), (), s32[]{:S(2)}) async-start(), calls=%async_computation.24 | async-start | bytes 28311552 | tf_op jit(solution)/shard_map/psum | solution.py:376
  664.2 4.6 copy-start.7
  664.2 4.6 copy-start.9
  679.7 4.4 copy-start.26
  690.1 169.6 %copy-start.90 = (f32[3,64]{1,0:T(4,128)S(1)}, f32[3,64]{1,0:T(4,128)}, u32[]{:S(2)}) copy-start(f32[3,64]{1,0:T(4,128)} %get-tuple-element.224) | copy-start | bytes 2308
  690.1 169.6 %copy-start.95 = (f32[3,64]{1,0:T(4,128)S(1)}, f32[3,64]{1,0:T(4,128)}, u32[]{:S(2)}) copy-start(f32[3,64]{1,0:T(4,128)} %get-tuple-element.226) | copy-start | bytes 2308
  690.1 169.8 %copy-start.94 = (f32[1,2,192]{2,1,0:T(2,128)S(1)}, f32[1,2,192]{2,1,0:T(2,128)}, u32[]{:S(2)}) copy-start(f32[1,2,192]{2,1,0:T(2,128)} %maximum_bitcast_fusion.10) | copy-start | bytes 4612
  690.1 169.8 %copy-start.67 = (f32[2,768]{1,0:T(2,128)S(1)}, f32[2,768]{1,0:T(2,128)}, u32[]{:S(2)}) copy-start(f32[2,768]{1,0:T(2,128)} %pad_maximum_fusion.8) | copy-start | bytes 18436
  690.1 211.1 %copy-start.44 = (f32[768]{0:T(1024)S(1)}, f32[768]{0:T(1024)}, u32[]{:S(2)}) copy-start(f32[768]{0:T(1024)} %copy-done.43) | copy-start | bytes 9220
  690.1 211.1 %copy-start.58 = (f32[256]{0:T(256)S(1)}, f32[256]{0:T(256)}, u32[]{:S(2)}) copy-start(f32[256]{0:T(256)} %copy-done.57) | copy-start | bytes 3076
  690.1 211.1 %copy-start.69 = (f32[256]{0:T(256)S(1)}, f32[256]{0:T(256)}, u32[]{:S(2)}) copy-start(f32[256]{0:T(256)} %copy-done.68) | copy-start | bytes 3076
  690.1 212.6 %copy-start.87 = (f32[1,768]{1,0:T(1,128)S(1)}, f32[1,768]{1,0:T(1,128)}, u32[]{:S(2)}) copy-start(f32[1,768]{1,0:T(1,128)} %stack.215) | copy-start | bytes 9220
  690.1 212.6 %copy-start.88 = (f32[1,768]{1,0:T(1,128)S(1)}, f32[1,768]{1,0:T(1,128)}, u32[]{:S(2)}) copy-start(f32[1,768]{1,0:T(1,128)} %stack.224) | copy-start | bytes 9220
  690.1 212.6 %copy-start.64 = (f32[1,2,768]{2,1,0:T(2,128)S(1)}, f32[1,2,768]{2,1,0:T(2,128)}, u32[]{:S(2)}) copy-start(f32[1,2,768]{2,1,0:T(2,128)} %maximum_bitcast_fusion.2) | copy-start | bytes 18436
  690.1 212.6 %copy-start.65 = (f32[1,2,768]{2,1,0:T(2,128)S(1)}, f32[1,2,768]{2,1,0:T(2,128)}, u32[]{:S(2)}) copy-start(f32[1,2,768]{2,1,0:T(2,128)} %maximum_bitcast_fusion.4) | copy-start | bytes 18436
  690.2 212.6 %copy-start.54 = (f32[2,2,768]{2,1,0:T(2,128)S(1)}, f32[2,2,768]{2,1,0:T(2,128)}, u32[]{:S(2)}) copy-start(f32[2,2,768]{2,1,0:T(2,128)} %pad_maximum_fusion.7) | copy-start | bytes 36868
  690.2 253.1 %copy-start.12 = (f32[256,768]{1,0:T(8,128)S(1)}, f32[256,768]{1,0:T(8,128)}, u32[]{:S(2)}) copy-start(f32[256,768]{1,0:T(8,128)} %copy-done.11) | copy-start | bytes 2359300
  1132.6 5.4 slice-start.2
  1132.6 4.4 copy-start.34
  1132.6 5.4 slice-start.3
  1137.0 4.2 slice-start
  1138.0 5.7 copy-start.1
  (73 other events, 151.9 us)
Sparse Core Ops, SparseCore 0:
  13.3 22.3 all-gather.8
  172.7 30.8 reduce-scatter.8
  208.9 19.6 all-gather.10
  243.4 28.1 reduce-scatter.10
  275.8 19.6 all-gather.12
  315.5 28.1 reduce-scatter.12
  347.8 19.6 all-gather.14
  369.2 19.7 all-gather.16
  398.4 28.1 reduce-scatter.16
  429.0 28.1 reduce-scatter.14
  462.7 19.6 all-gather.18
  516.0 28.1 reduce-scatter.18
  551.0 19.6 all-gather.20
  580.1 28.1 reduce-scatter.20
  614.9 19.6 all-gather.22
  654.4 28.1 reduce-scatter.22
  689.5 443.0 all-reduce.4
where the time goes:
time: 1160 us; the launch traced here: 1150 us
  waiting for transfers between devices  468 us (40%)
  matrix products  388 us (33%)
  local copies, waits for them, and re-layouts  124 us (11%)
  blocking collectives  81.1 us (7%)
  other arithmetic  61.5 us (5%)
  between operations  15.7 us (1%)
  starting transfers between devices  12.5 us (1%)
    psum x1, waiting for transfers between devices, per_device(): lax.psum((qkv_all, qvb_all, out_all, up_all, upb_all, down_all, table_all...  187 us
    dot_general x24, matrix products, times_transposed(): lax.dot_general(left_side, right_side, (((1,), (1,)), ((), ())), preferre...  180 us
    dot_general x16, matrix products, one_block(): jnp.dot(columns, onehot, preferred_element_type=jnp.float32)  128 us
    reduce_scatter x4, waiting for transfers between devices, project_rows(): lax.psum_scatter(jnp.dot(left_side, right_side, preferred_element_type=jn...  113 us
    reduce_scatter x4, waiting for transfers between devices, project_grads(): lax.psum_scatter(times_transposed(left_side, right_side).astype(jnp.bfloa...  80.5 us
    all_gather x4, waiting for transfers between devices, spread_grads(): return lax.all_gather(values, 'tensor', axis=0, tiled=True)  45.9 us
    all_gather x4, waiting for transfers between devices, spread_rows(): return lax.all_gather(values, 'tensor', axis=0, tiled=True)  40.9 us
    psum x1, blocking collectives, per_device(): lax.psum((qkv_all, qvb_all, out_all, up_all, upb_all, down_all, table_all...  40.7 us
  transfers between devices with their start and end apart: 17, of which 14 were waited for; matrix products, arithmetic and copies ran while one was open for 35% of the time, Pallas kernels for 0%

commit v1 on v0

--- a/solution.py
+++ b/solution.py
@@ -377,8 +377,16 @@
         (qkv_all, qvb_all, out_all, up_all, upb_all, down_all, table_all), "dp"
     )
     gain_all, shift_all, scale_all, rowb_all = lax.psum(
-        (jnp.stack(list_gain), jnp.stack(list_shift), jnp.stack(list_scale), jnp.stack(list_rowb)),
-        ("dp", "tensor"),
+        lax.psum(
+            (
+                jnp.stack(list_gain),
+                jnp.stack(list_shift),
+                jnp.stack(list_scale),
+                jnp.stack(list_rowb),
+            ),
+            "tensor",
+        ),
+        "dp",
     )
     return (
         result,

time: 1160 us -> 1420 us (1.22)
  waiting for transfers between devices: 468 us -> 771 us
  blocking collectives: 81.1 us -> 11.2 us
    psum x1 -> x2, waiting for transfers between devices: 187 us -> 512 us  [per_device(): lax.psum((qkv_all, qvb_all, out_all, up_all, upb_all, down_all, table_all...]
    psum x1 -> x0, blocking collectives: 40.7 us -> none  [per_device(): lax.psum((qkv_all, qvb_all, out_all, up_all, upb_all, down_all, table_all...]
    psum x1, blocking collectives: 40.4 us -> 11.2 us  [per_device(): lax.psum((jnp.stack(list_gain), jnp.stack(list_shift), jnp.stack(list_sca...]
    reduce_scatter x4, waiting for transfers between devices: 80.5 us -> 56.9 us  [project_grads(): lax.psum_scatter(times_transposed(left_side, right_side).astype(jnp.bfloa...]
    unnamed x254 -> x260, local copies, waits for them, and re-layouts: 36.6 us -> 39.4 us
  transfers between devices with their start and end apart: 17 -> 18, of which waited for: 14 -> 16; matrix products, arithmetic and copies ran while one was open for 35% -> 30% of each run, Pallas kernels for 0% -> 0%
where the time goes in v1:
time: 1420 us; the launch traced here: 1410 us
  waiting for transfers between devices  771 us (54%)
  matrix products  400 us (28%)
  local copies, waits for them, and re-layouts  131 us (9%)
  other arithmetic  63.3 us (4%)
  between operations  16 us (1%)
    psum x2, waiting for transfers between devices, per_device(): lax.psum((qkv_all, qvb_all, out_all, up_all, upb_all, down_all, table_all...  512 us
    dot_general x24, matrix products, times_transposed(): lax.dot_general(left_side, right_side, (((1,), (1,)), ((), ())), preferre...  191 us
    dot_general x16, matrix products, one_block(): jnp.dot(columns, onehot, preferred_element_type=jnp.float32)  128 us
    reduce_scatter x4, waiting for transfers between devices, project_rows(): lax.psum_scatter(jnp.dot(left_side, right_side, preferred_element_type=jn...  113 us
    reduce_scatter x4, waiting for transfers between devices, project_grads(): lax.psum_scatter(times_transposed(left_side, right_side).astype(jnp.bfloa...  56.9 us
    all_gather x4, waiting for transfers between devices, spread_grads(): return lax.all_gather(values, 'tensor', axis=0, tiled=True)  47.9 us
    all_gather x4, waiting for transfers between devices, spread_rows(): return lax.all_gather(values, 'tensor', axis=0, tiled=True)  41 us
    unnamed x260, local copies, waits for them, and re-layouts  39.4 us
  transfers between devices with their start and end apart: 18, of which 16 were waited for; matrix products, arithmetic and copies ran while one was open for 30% of the time, Pallas kernels for 0%

profile of v1, /device:TPU:0, one launch (start us, length us, event | category | flops | bytes accessed | tf_op | source)
XLA Modules:
  0.0 1406.7 jit_solution(11211086813413113507)
XLA Ops:
  15.4 128.6 %while.22 = (s32[]{:T(128)}, bf16[16,6,16384]{2,1,0:T(8,128)(2,1)}, s32[16,16384]{1,0:T(8,128)S(1)}, bf16[6,732]{1,0:T(8,128)(2,1)S(1)}, s32[]{:T(128)}) while((s32[]{:T(128)}, bf16[16,6,16384]{2,1,0:T(8,128)(2,1)}, s32[16,16384]{1,0:T(8,128)S(1)}, bf16[6,732]{1,0:T(8,128)(2,1)S(1)}, s32[]{:T(128)}) %tuple.112), condition=%wide.region_4.5_spmd.clone, body=%wide.region_3.4_spmd.clone.sunk | while | flops 156008448 | bytes 467613 | solution.py:62
  15.5 8.0 fusion.241
  23.5 8.0 fusion.241
  31.5 8.0 fusion.241
  39.6 8.0 fusion.241
  47.6 8.0 fusion.241
  55.7 8.0 fusion.241
  63.7 8.0 fusion.241
  71.7 8.0 fusion.241
  79.8 8.0 fusion.241
  87.8 8.0 fusion.241
  95.8 8.0 fusion.241
  103.9 8.0 fusion.241
  111.9 8.0 fusion.241
  119.9 8.0 fusion.241
  128.0 8.0 fusion.241
  136.0 8.0 fusion.241
  145.5 3.9 copy.54
  152.8 5.0 copy.55
  174.2 29.5 %reduce-scatter.9.cloned.1.call-done = bf16[256,768]{1,0:T(8,128)(2,1)} async-done(((bf16[1024,768]{1,0:T(8,128)(2,1)}), bf16[256,768]{1,0:T(8,128)(2,1)}) %reduce-scatter.9.cloned.1.call-update) | async-done | bytes 393232 | tf_op jit(solution)/shard_map/reduce_scatter | solution.py:231
  210.2 18.4 %all-gather.11.cloned.1.call-done = bf16[1024,768]{1,0:T(8,128)(2,1)} async-done(((bf16[256,768]{1,0:T(8,128)(2,1)}), bf16[1024,768]{1,0:T(8,128)(2,1)}) %all-gather.11.cloned.1.call-update) | async-done | bytes 1572880 | tf_op jit(solution)/shard_map/all_gather | solution.py:225
  228.7 11.0 fusion.17
  243.4 28.3 %reduce-scatter.11.cloned.1.call-done = bf16[256,768]{1,0:T(8,128)(2,1)} async-done(((bf16[1024,768]{1,0:T(8,128)(2,1)}), bf16[256,768]{1,0:T(8,128)(2,1)}) %reduce-scatter.11.cloned.1.call-update) | async-done | bytes 393232 | tf_op jit(solution)/shard_map/reduce_scatter | solution.py:231
  275.7 11.0 reduce-scatter.13.cloned.1.call-start
  289.4 6.2 all-gather.13.cloned.1.call-done
  315.5 28.3 %reduce-scatter.13.cloned.1.call-done = bf16[256,768]{1,0:T(8,128)(2,1)} async-done(((bf16[1024,768]{1,0:T(8,128)(2,1)}), bf16[256,768]{1,0:T(8,128)(2,1)}) %reduce-scatter.13.cloned.1.call-update) | async-done | bytes 393232 | tf_op jit(solution)/shard_map/reduce_scatter | solution.py:231
  351.2 16.4 %all-gather.15.cloned.1.call-done = bf16[1024,768]{1,0:T(8,128)(2,1)} async-done(((bf16[256,768]{1,0:T(8,128)(2,1)}), bf16[1024,768]{1,0:T(8,128)(2,1)}) %all-gather.15.cloned.1.call-update) | async-done | bytes 1572880 | tf_op jit(solution)/shard_map/all_gather | solution.py:225
  367.6 11.2 fusion.20
  378.9 10.1 all-gather.17.cloned.1.call-done
  389.0 5.6 convert_reduce_fusion
  398.4 4.3 convolution_convert_fusion.4
  402.7 23.9 %reduce-scatter.17.cloned.1.call-done = bf16[256,768]{1,0:T(8,128)(2,1)} async-done(((bf16[1024,768]{1,0:T(8,128)(2,1)}), bf16[256,768]{1,0:T(8,128)(2,1)}) %reduce-scatter.17.cloned.1.call-update) | async-done | bytes 393232 | tf_op jit(solution)/shard_map/reduce_scatter | solution.py:239
  430.0 27.2 %reduce-scatter.15.cloned.1.call-done = bf16[256,768]{1,0:T(8,128)(2,1)} async-done(((bf16[1024,768]{1,0:T(8,128)(2,1)}), bf16[256,768]{1,0:T(8,128)(2,1)}) %reduce-scatter.15.cloned.1.call-update) | async-done | bytes 393232 | tf_op jit(solution)/shard_map/reduce_scatter | solution.py:231
  466.5 15.9 %all-gather.19.cloned.1.call-done = bf16[1024,768]{1,0:T(8,128)(2,1)} async-done(((bf16[256,768]{1,0:T(8,128)(2,1)}), bf16[1024,768]{1,0:T(8,128)(2,1)}) %all-gather.19.cloned.1.call-update) | async-done | bytes 1572880 | tf_op jit(solution)/shard_map/all_gather | solution.py:228
  516.0 28.3 %reduce-scatter.19.cloned.1.call-done = bf16[256,768]{1,0:T(8,128)(2,1)} async-done(((bf16[1024,768]{1,0:T(8,128)(2,1)}), bf16[256,768]{1,0:T(8,128)(2,1)}) %reduce-scatter.19.cloned.1.call-update) | async-done | bytes 393232 | tf_op jit(solution)/shard_map/reduce_scatter | solution.py:239
  551.0 19.8 %all-gather.21.cloned.1.call-done = bf16[1024,768]{1,0:T(8,128)(2,1)} async-done(((bf16[256,768]{1,0:T(8,128)(2,1)}), bf16[1024,768]{1,0:T(8,128)(2,1)}) %all-gather.21.cloned.1.call-update) | async-done | bytes 1572880 | tf_op jit(solution)/shard_map/all_gather | solution.py:228
  570.8 5.6 convert_reduce_fusion.1
  582.3 4.9 convolution_bitcast_fusion.2
  597.9 4.1 fusion.72
  603.7 4.7 reduce-scatter.21.cloned.1.call-done
  649.3 3.9 convolution_convert_fusion
  655.5 4.8 copy.81
  660.3 4.3 reshape.401
  668.3 179.0 %while.23 = (s32[]{:T(128)}, f32[6,732]{1,0:T(8,128)}, bf16[16,6,16384]{2,1,0:T(8,128)(2,1)}, s32[16,16384]{1,0:T(8,128)}, s32[]{:T(128)}, /*index=5*/s32[]{:T(128)}) while((s32[]{:T(128)}, f32[6,732]{1,0:T(8,128)}, bf16[16,6,16384]{2,1,0:T(8,128)(2,1)}, s32[16,16384]{1,0:T(8,128)}, s32[]{:T(128)}, /*index=5*/s32[]{:T(128)}) %tuple.157), condition=%wide.region_46.47_spmd.clone, body=%wide.region_45.46_spmd.clone.sunk | while | flops 155918912 | bytes 500991 | solution.py:89
  669.4 10.1 fusion.243
  680.6 10.1 fusion.243
  691.8 10.1 fusion.243
  703.0 10.1 fusion.243
  714.1 10.1 fusion.243
  725.3 10.1 fusion.243
  736.5 10.1 fusion.243
  747.7 10.1 fusion.243
  758.8 10.1 fusion.243
  770.0 10.1 fusion.243
  781.2 10.1 fusion.243
  792.3 10.1 fusion.243
  803.5 10.1 fusion.243
  814.7 10.1 fusion.243
  825.9 10.1 fusion.243
  837.0 10.1 fusion.243
  856.8 11.2 all-reduce.2
  871.6 68.3 %all-reduce.6.cloned.1.call-done = (f32[2,2,192]{2,1,0:T(2,128)}, f32[2,768]{1,0:T(2,128)}, f32[2,732,3]{1,2,0:T(4,128)}, f32[2,2,768]{2,1,0:T(2,128)}, f32[2,2,...) async-done(((f32[2,2,192]{2,1,0:T(2,128)}, f32[2,768]{1,0:T(2,128)}, f32[2,732,3]{1,2,0:T(4,128)}, f32[2,2,768]{2,1,0:T(2,128)}, f32[2,2,768]{2,1,0:T(2,128)}, ...) | async-done | bytes 75952 | tf_op jit(solution)/shard_map/psum | solution.py:376
  941.3 444.0 %all-reduce.8.cloned.1.call-done = (f32[2,768,3,192]{1,3,2,0:T(8,128)}, f32[2,192,768]{2,1,0:T(8,128)}, f32[2,768,768]{2,1,0:T(8,128)}, f32[2,768,768]{2,1,0:T(8,128)}) async-done(((f32[2,768,3,192]{1,3,2,0:T(8,128)}, f32[2,192,768]{2,1,0:T(8,128)}, f32[2,768,768]{2,1,0:T(8,128)}, f32[2,768,768]{2,1,0:T(8,128)}), (f32[2,768,3,192]{1,3,2,0:T(8,128)}, f32[2,192,768]{2,1,0:T(8,128)}, f32[2,768,768]{2,1,0:T(8,128)}, ...) | async-done | bytes 14155792 | tf_op jit(solution)/shard_map/psum | solution.py:376
  1385.2 4.3 copy.183
  (495 shorter events, 237.1 us)
Async XLA Ops:
  7.2 340.7 %copy-start = (s32[4,2]{0,1:T(2,128)S(1)}, s32[4,2]{0,1:T(2,128)}, u32[]{:S(2)}) copy-start(s32[4,2]{0,1:T(2,128)} %param.23) | copy-start | bytes 100
  7.2 151.5 %all-gather.9.cloned.1.call-start = ((), (), s32[]{:S(2)}) async-start(), calls=%async_computation.8 | async-start | bytes 1966080 | tf_op jit(solution)/shard_map/all_gather | solution.py:225
  8.4 4.8 copy-start.56
  13.2 190.5 %reduce-scatter.9.cloned.1.call-start = ((), (), s32[]{:S(2)}) async-start(), calls=%async_computation.9 | async-start | bytes 1966080 | tf_op jit(solution)/shard_map/reduce_scatter | solution.py:231
  15.4 128.6 %copy-start.102 = (s32[1024]{0:T(1024)S(1)}, s32[1024]{0:T(1024)}, u32[]{:S(2)}) copy-start(s32[1024]{0:T(1024)} %param.22) | copy-start | bytes 12292
  15.4 128.6 %copy-start.104 = (bf16[2,2,192]{2,1,0:T(2,128)(2,1)S(1)}, bf16[2,2,192]{2,1,0:T(2,128)(2,1)}, u32[]{:S(2)}) copy-start(bf16[2,2,192]{2,1,0:T(2,128)(2,1)} %param.26) | copy-start | bytes 4612
  144.8 20.2 %copy-start.91 = (f32[3,64]{1,0:T(4,128)}, f32[3,64]{1,0:T(4,128)S(1)}, u32[]{:S(2)}) copy-start(f32[3,64]{1,0:T(4,128)S(1)} %add.315) | copy-start | bytes 2308
  152.8 5.9 copy-start.30
  169.7 33.9 %copy-start.4 = (bf16[256,768]{1,0:T(8,128)(2,1)S(1)}, bf16[256,768]{1,0:T(8,128)(2,1)}, u32[]{:S(2)}) copy-start(bf16[256,768]{1,0:T(8,128)(2,1)} %param.20) | copy-start | bytes 1179652
  172.7 56.0 %all-gather.11.cloned.1.call-start = ((), (), s32[]{:S(2)}) async-start(), calls=%async_computation.10 | async-start | bytes 1966080 | tf_op jit(solution)/shard_map/all_gather | solution.py:225
  208.8 62.9 %reduce-scatter.11.cloned.1.call-start = ((), (), s32[]{:S(2)}) async-start(), calls=%async_computation.11 | async-start | bytes 1966080 | tf_op jit(solution)/shard_map/reduce_scatter | solution.py:231
  228.7 12.1 copy-start.106
  243.3 52.2 %all-gather.13.cloned.1.call-start = ((), (), s32[]{:S(2)}) async-start(), calls=%async_computation.12 | async-start | bytes 1966080 | tf_op jit(solution)/shard_map/all_gather | solution.py:225
  275.7 68.1 %reduce-scatter.13.cloned.1.call-start = ((), (), s32[]{:S(2)}) async-start(), calls=%async_computation.13 | async-start | bytes 1966080 | tf_op jit(solution)/shard_map/reduce_scatter | solution.py:231
  315.5 52.1 %all-gather.15.cloned.1.call-start = ((), (), s32[]{:S(2)}) async-start(), calls=%async_computation.14 | async-start | bytes 1966080 | tf_op jit(solution)/shard_map/all_gather | solution.py:225
  347.8 41.2 %all-gather.17.cloned.1.call-start = ((), (), s32[]{:S(2)}) async-start(), calls=%async_computation.16 | async-start | bytes 1966080 | tf_op jit(solution)/shard_map/all_gather | solution.py:228
  349.2 18.4 %copy-start.105 = (pred[256]{0:T(512)(128)(4,1)}, pred[256]{0:T(512)(128)(4,1)S(1)}, u32[]{:S(2)}) copy-start(pred[256]{0:T(512)(128)(4,1)S(1)} %dynamic_slice.14) | copy-start | bytes 772
  351.1 75.5 %reduce-scatter.17.cloned.1.call-start = ((), (), s32[]{:S(2)}) async-start(), calls=%async_computation.17 | async-start | bytes 1966080 | tf_op jit(solution)/shard_map/reduce_scatter | solution.py:239
  367.6 21.4 %copy-start.100 = (f32[768]{0:T(1024)S(1)}, f32[768]{0:T(1024)}, u32[]{:S(2)}) copy-start(f32[768]{0:T(1024)} %get-tuple-element.153) | copy-start | bytes 9220
  389.0 6.7 copy-start.107
  398.3 58.9 %reduce-scatter.15.cloned.1.call-start = ((), (), s32[]{:S(2)}) async-start(), calls=%async_computation.15 | async-start | bytes 1966080 | tf_op jit(solution)/shard_map/reduce_scatter | solution.py:231
  398.4 28.3 %copy-start.45 = (f32[768]{0:T(1024)S(1)}, f32[768]{0:T(1024)}, u32[]{:S(2)}) copy-start(f32[768]{0:T(1024)} %get-tuple-element.239) | copy-start | bytes 9220
  402.7 79.7 %all-gather.19.cloned.1.call-start = ((), (), s32[]{:S(2)}) async-start(), calls=%async_computation.18 | async-start | bytes 1966080 | tf_op jit(solution)/shard_map/all_gather | solution.py:228
  457.2 4.5 copy-start.55
  462.6 81.7 %reduce-scatter.19.cloned.1.call-start = ((), (), s32[]{:S(2)}) async-start(), calls=%async_computation.19 | async-start | bytes 1966080 | tf_op jit(solution)/shard_map/reduce_scatter | solution.py:239
  466.5 24.2 %copy-start.98 = (f32[3,64]{1,0:T(4,128)S(1)}, f32[3,64]{1,0:T(4,128)}, u32[]{:S(2)}) copy-start(f32[3,64]{1,0:T(4,128)} %add.339) | copy-start | bytes 2308
  512.2 32.1 %copy-start.44 = (f32[768]{0:T(1024)S(1)}, f32[768]{0:T(1024)}, u32[]{:S(2)}) copy-start(f32[768]{0:T(1024)} %get-tuple-element.236) | copy-start | bytes 9220
  516.0 54.8 %all-gather.21.cloned.1.call-start = ((), (), s32[]{:S(2)}) async-start(), calls=%async_computation.20 | async-start | bytes 1966080 | tf_op jit(solution)/shard_map/all_gather | solution.py:228
  544.3 5.8 copy-start.54
  551.0 57.4 %reduce-scatter.21.cloned.1.call-start = ((), (), s32[]{:S(2)}) async-start(), calls=%async_computation.21 | async-start | bytes 1966080 | tf_op jit(solution)/shard_map/reduce_scatter | solution.py:239
  570.8 6.7 copy-start.108
  577.5 4.2 copy-start.101
  580.1 54.5 %all-gather.23.cloned.1.call-start = ((), (), s32[]{:S(2)}) async-start(), calls=%async_computation.22 | async-start | bytes 1966080 | tf_op jit(solution)/shard_map/all_gather | solution.py:228
  582.3 4.9 copy-start.110
  582.3 4.9 copy-start.112
  587.2 4.0 copy-start.77
  587.2 4.0 copy-start.76
  597.8 4.1 copy-start.79
  597.8 4.7 copy-start.80
  597.9 5.3 copy-start.78
  597.9 10.6 copy-start.59
  614.8 240.3 %reduce-scatter.23.cloned.1.call-start = ((), (), s32[]{:S(2)}) async-start(), calls=%async_computation.23 | async-start | bytes 1966080 | tf_op jit(solution)/shard_map/reduce_scatter | solution.py:239
  628.1 3.8 copy-start.52
  628.1 3.7 copy-start.70
  628.1 3.7 copy-start.71
  628.1 3.7 copy-start.72
  628.1 3.7 copy-start.73
  628.1 3.8 copy-start.90
  628.1 3.8 copy-start.64
  649.3 4.2 copy-start.7
  649.3 4.2 copy-start.9
  653.3 286.6 %all-reduce.6.cloned.1.call-start = ((), (), s32[]{:S(2)}) async-start(), calls=%async_computation.24 | async-start | bytes 167936 | tf_op jit(solution)/shard_map/psum | solution.py:376
  668.3 179.1 %copy-start.95 = (f32[3,64]{1,0:T(4,128)S(1)}, f32[3,64]{1,0:T(4,128)}, u32[]{:S(2)}) copy-start(f32[3,64]{1,0:T(4,128)} %get-tuple-element.230) | copy-start | bytes 2308
  668.3 180.7 %copy-start.94 = (f32[1,2,192]{2,1,0:T(2,128)S(1)}, f32[1,2,192]{2,1,0:T(2,128)}, u32[]{:S(2)}) copy-start(f32[1,2,192]{2,1,0:T(2,128)} %maximum_bitcast_fusion.10) | copy-start | bytes 4612
  847.3 5.1 copy-start.29
  854.6 13.5 copy-start.26
  868.0 517.2 %all-reduce.8.cloned.1.call-start = ((), (), s32[]{:S(2)}) async-start(), calls=%async_computation.25 | async-start | bytes 28311552 | tf_op jit(solution)/shard_map/psum | solution.py:376
  1385.2 6.0 slice-start.2
  1385.2 4.4 copy-start.103
  1385.2 5.0 copy-start.35
  1385.2 6.0 slice-start.3
  1390.2 4.6 slice-start
  1394.2 5.2 copy-start.1
  1394.8 4.0 copy-start.84
  (74 other events, 140.5 us)
Sparse Core Ops, SparseCore 0:
  13.3 22.3 all-gather.8
  172.8 30.8 reduce-scatter.8
  208.9 19.6 all-gather.10
  243.5 28.1 reduce-scatter.10
  275.8 19.6 all-gather.12
  315.6 28.1 reduce-scatter.12
  347.9 19.6 all-gather.14
  369.2 19.7 all-gather.16
  398.4 28.1 reduce-scatter.16
  429.0 28.1 reduce-scatter.14
  462.7 19.6 all-gather.18
  516.1 28.1 reduce-scatter.18
  551.1 19.6 all-gather.20
  580.2 28.1 reduce-scatter.20
  614.9 19.6 all-gather.22
  653.4 28.1 reduce-scatter.22
  868.2 71.7 all-reduce.5
  945.0 440.1 all-reduce.7
